TPU v7x, 32 devices: a whole 2x2x4 slice. The times are simulated.
32 devices in a mesh: member: 2 (over x), lateral: 8 (over z, y), radial: 2 (over core).
Axes of the slice: x: 2, y: 2, z: 4, core: 2. Of those that a mesh axis runs over, the one named last changes fastest.
Arguments:
- initial_displacement: float32 [6, 8, 256, 2048], P('member', 'radial', 'lateral'), parts along dimension 0, may hold values from -6 to 6
- force: float32 [6, 8, 256, 2048], P('member', 'radial', 'lateral'), parts along dimension 0, may hold values from -12 to 12
- viscosity: float32 [32], P('member'), parts along dimension 0, may hold values from 0.1 to 10
- layer_index: int32 [8, 256, 2048], P('radial', 'lateral'), may hold values from 0 to 15
- response: float32 [512, 1024], P(None, 'lateral'), may hold values from 0.2 to 2
- ocean_mask: int32 [256, 2048], P('lateral'), may hold values 0 or 1
Outputs:
- displacement: float32 [6, 8, 256, 2048], P('member', 'radial', 'lateral'), parts along dimension 0
- coefficients: float32 [1024, 1024], P('member', ('lateral', 'radial')), parts along dimension 0
- sea_load: float32 [256, 4096], P('lateral', 'member'), parts along dimension 1
There are 2 independent parts, one for each index of `member`. A program takes and returns all parts, laid end to end along the dimension named above; an argument that names none is the same for every part. Nothing has to cross between parts.
All inputs are finite; a program needn't handle non-finite values. No bound on the sum of `ocean_mask` on one device may be relied on, other than what follows from the above.
Results may differ from a plain program's by a relative error of at most 0.000073.
Values sent between devices are 32-bit elements; how exact they have to be, the bound alone decides.
A program may use at most 128 MiB of HBM per device.

v0:
```python
import functools
import math

import jax
import jax.numpy as jnp
import ml_dtypes
import numpy as np
from jax import lax
from jax.experimental import pallas as pl
from jax.experimental.pallas import tpu as pltpu
from jax.sharding import PartitionSpec as P

MODES = 512
PAD = 8
VMEM = 67043328
MESH = pl.DeviceIdType.MESH
f32, bf16 = jnp.float32, jnp.bfloat16


def halves(table):
    table = table.astype(np.float32)
    high = table.astype(ml_dtypes.bfloat16)
    low = (table - high.astype(np.float32)).astype(ml_dtypes.bfloat16)
    return high, low


def longitude_quarter(count, modes):
    points = np.arange(count // 4)[:, None]
    phase = points * np.arange(modes)[None, :] % count
    angle = 2.0 * math.pi / count * phase
    table = np.concatenate([np.cos(angle), np.sin(angle)], axis=1)
    return halves(table * math.sqrt(2.0 / count))


def colatitude_table(count, modes):
    points = np.arange(count)[:, None]
    phase = np.arange(modes)[None, :] * (2 * points + 1) % (4 * count)
    table = np.cos(math.pi / (2 * count) * phase) * math.sqrt(2.0 / count)
    return halves(table)


def split(x):
    high = x.astype(bf16)
    return high, (x - high.astype(f32)).astype(bf16)


def dot(a, b, dims=(((1,), (0,)), ((), ()))):
    return lax.dot_general(a, b, dims, preferred_element_type=f32)


def choose(index, values):
    bit = 0
    while len(values) > 1:
        odd = (index & (1 << bit)) != 0
        values = [
            jnp.where(odd, values[min(i + 1, len(values) - 1)], values[i])
            for i in range(0, len(values), 2)
        ]
        bit += 1
    return values[0]


def kernel(lat, rad, layers, disp, force, visc, layer, response, mask, th, tl, ch, cl,
           out, coef_out, gather, th_v, tl_v, mask_v,
           u0, u1, fv, fh, li, he, fsend, frecv, gsend, grecv, resp_v, resp_t, ch_v, cl_v, visc_s,
           load_sem, x_send, x_recv, r_send, r_recv, a_send, a_recv, b_send, b_recv, far_sem):
    comps, shells, rows, lon = disp.shape
    width = response.shape[1]
    me = lax.axis_index("lateral")
    place = lax.axis_index("radial")
    inner = pl.ds(PAD, rows)
    last = shells - 1
    top = place == rad - 1
    south, north = me < lat - 1, me > 0
    face = jnp.where(top, 0, last)

    def order(i):
        return jnp.where(top, last - i, i)

    def load(source, target, index):
        copy = pltpu.make_async_copy(source, target, load_sem.at[index])
        copy.start()
        return copy

    def field(c):
        return u0.at[c, pl.ds(1, shells), inner]

    def around(d, e):
        return {"lateral": lax.rem(me + d, lat), "radial": lax.rem(place + e, rad)}

    offsets = [(d, e) for d in range(lat) for e in range(rad) if d or e]
    barrier = pltpu.get_barrier_semaphore()
    for e in range(1, rad):
        pl.semaphore_signal(barrier, inc=1, device_id=around(0, e), device_id_type=MESH)

    def greet(sem, step):
        @pl.when(me + step < lat)
        def _():
            pl.semaphore_signal(sem, inc=1, device_id={"lateral": me + step}, device_id_type=MESH)

        @pl.when(me >= step)
        def _():
            pl.semaphore_signal(sem, inc=1, device_id={"lateral": me - step}, device_id_type=MESH)

    def greeted(step):
        return jnp.where(me + step < lat, 1, 0) + jnp.where(me >= step, 1, 0)

    greet(barrier, 1)
    steps = [1 << k for k in range((lat - 1).bit_length())]

    c_visc = load(visc, visc_s, 0)
    c_layer = load(layer, li.at[pl.ds(1, shells), inner], 1)
    c_disp, c_force = [], []
    for c in range(comps):
        c_disp.append(load(disp.at[c], field(c), 2 + 2 * c))
        c_force.append(load(force.at[c], fv.at[c], 3 + 2 * c))

    void = jnp.where(top, shells + 1, 0)
    tall, wide = rows + 2 * PAD, (1, lon)
    he[void] = jnp.zeros((tall, lon), f32)
    for c in range(comps):
        u0[c, void] = jnp.zeros((tall, lon), f32)
        u1[c, void] = jnp.zeros((tall, lon), f32)

    def unpadded(row):
        for s in range(1, shells + 1):
            he[s, row:row + 1, :] = jnp.zeros(wide, f32)
            for c in range(comps):
                u0[c, s, row:row + 1, :] = jnp.zeros(wide, f32)
                u1[c, s, row:row + 1, :] = jnp.zeros(wide, f32)

    @pl.when(jnp.logical_not(north))
    def _():
        unpadded(PAD - 1)

    @pl.when(jnp.logical_not(south))
    def _():
        unpadded(PAD + rows)

    sides = [
        (0, south, north, jnp.where(south, me + 1, me), pl.ds(rows - 1, 1), pl.ds(rows - 2, 2),
         pl.ds(PAD - 1, 1), pl.ds(PAD - 2, 2), pl.ds(PAD + rows - 1, 1)),
        (1, north, south, jnp.where(north, me - 1, me), pl.ds(0, 1), pl.ds(0, 2),
         pl.ds(PAD + rows, 1), pl.ds(PAD + rows, 2), pl.ds(PAD, 1)),
    ]

    def lateral(side, k, source, target):
        return pltpu.make_async_remote_copy(
            src_ref=source, dst_ref=target, send_sem=x_send.at[side[0], k], recv_sem=x_recv.at[side[0], k],
            device_id={"lateral": side[3]}, device_id_type=MESH)

    def first(side):
        _, _, _, _, one, two, edge, pair, _ = side
        refs = [
            (disp.at[0, last, two], u0.at[0, shells, pair]),
            (layer.at[last, two], li.at[shells, pair]),
            (disp.at[0, last - 1, one], u0.at[0, shells - 1, edge]),
            (layer.at[last - 1, one], li.at[shells - 1, edge]),
            (force.at[0, last, one], fh.at[side[0]]),
        ]
        return [lateral(side, k, a, b) for k, (a, b) in enumerate(refs)]

    rest = pl.ds(1, comps - 1)

    def bulk_rest(side, i):
        s = order(i)
        return [lateral(side, 5 + i, disp.at[rest, s, side[4]], u0.at[rest, s + 1, side[6]])]

    def bulk_all(side, i):
        s = order(i)
        return [lateral(side, 5 + shells + i, layer.at[s, side[4]], li.at[s + 1, side[6]]),
                lateral(side, 5 + i, disp.at[:, s, side[4]], u0.at[:, s + 1, side[6]])]

    def later_rest(side, i):
        s = order(i)
        return [lateral(side, 5 + 2 * shells + i, u1.at[rest, s + 1, side[8]], u1.at[rest, s + 1, side[6]])]

    def later_all(side, i):
        s = order(i)
        return [lateral(side, 5 + 2 * shells + i, u1.at[:, s + 1, side[8]], u1.at[:, s + 1, side[6]])]

    def for_shell(i, act, some, every):
        alone = jnp.logical_and(top, i < some[1])

        @pl.when(alone)
        def _():
            act(some[0])

        @pl.when(jnp.logical_not(alone))
        def _():
            act(every)

    def start_to(i, some, every):
        for side in sides:
            @pl.when(side[1])
            def _():
                for_shell(i, lambda make: [c.start() for c in make(side, i)], some, every)

    def sent_to(i, some, every):
        for side in sides:
            @pl.when(side[1])
            def _():
                for_shell(i, lambda make: [c.wait_send() for c in make(side, i)], some, every)

    def got_from(i, some, every):
        for side in sides:
            @pl.when(side[2])
            def _():
                for_shell(i, lambda make: [c.wait_recv() for c in make(side, i)], some, every)

    bulk = ((bulk_rest, 2), bulk_all)
    later = ((later_rest, 1), later_all)

    def across(k, source, target):
        return pltpu.make_async_remote_copy(
            src_ref=source, dst_ref=target, send_sem=r_send.at[k], recv_sem=r_recv.at[k],
            device_id={"radial": rad - 1 - place}, device_id_type=MESH)

    beyond = jnp.where(top, shells + 1, 0)
    facing = jnp.where(top, 0, shells + 1)
    r_layer = across(0, layer.at[face], li.at[beyond, inner])
    r_disp = across(1, disp.at[:, face], u0.at[:, beyond, inner])
    r_later = across(2, u1.at[:, face + 1, inner], u1.at[:, beyond, inner])

    pl.semaphore_wait(barrier, greeted(1) + rad - 1)

    @pl.when(top)
    def _():
        for side in sides:
            @pl.when(side[1])
            def _():
                for copy in first(side):
                    copy.start()

    r_layer.start()
    r_disp.start()
    greet(far_sem.at[0], steps[0])

    @pl.when(top)
    def _():
        for i in range(shells):
            start_to(i, *bulk)

    c_visc.wait()
    values = [visc_s[i] * 0.5 for i in range(layers)]

    def lookup_at(s, where):
        he[s, where, :] = choose(li[s, where, :], values)

    def lookup(s):
        for r in range(0, rows, 8):
            lookup_at(s, pl.ds(PAD + r, 8))

    def lookup_step(i, carry):
        lookup(order(i) + 1)
        return carry

    c_layer.wait()
    lax.fori_loop(0, shells, lookup_step, 0)

    @pl.when(jnp.logical_not(top))
    def _():
        for i in range(shells):
            start_to(i, *bulk)

    tables = [(th, th_v), (tl, tl_v), (response, resp_v), (ch, ch_v), (cl, cl_v), (mask, mask_v)]
    for copy in c_disp + c_force:
        copy.wait()
    c_tables = [load(a, b, 2 + 2 * comps + k) for k, (a, b) in enumerate(tables)]

    for k, step in enumerate(steps):
        if k:
            pl.semaphore_wait(far_sem.at[k - 1], greeted(steps[k - 1]))
            greet(far_sem.at[k], step)
            break

    chunk = lon // 4

    def beside(load, k):
        first, end = k * chunk, (k + 1) * chunk
        mid = load(slice(first, end))
        before = load(slice((first - 128) % lon, (first - 128) % lon + 128))
        after = load(slice(end % lon, end % lon + 128))
        left = pltpu.roll(jnp.concatenate([before, mid], axis=1), 1, 1)[:, 128:]
        right = pltpu.roll(jnp.concatenate([mid, after], axis=1), chunk + 127, 1)[:, :chunk]
        return mid, left, right

    def sweep(src, s, r, size, some, pushed, store):
        here, next_row, last_row = slice(r, r + size), slice(r + 1, r + size + 1), slice(r - 1, r + size - 1)
        for k in range(4):
            lanes = slice(k * chunk, (k + 1) * chunk)
            h, left, right = beside(lambda cols: he[s + 1, here, cols], k)
            ws = [
                h + he[s + 2, here, lanes],
                h + he[s, here, lanes],
                h + he[s + 1, next_row, lanes],
                h + he[s + 1, last_row, lanes],
                h + left,
                h + right,
            ]
            rate = 0.8 / (1.0 + (((ws[0] + ws[1]) + (ws[2] + ws[3])) + (ws[4] + ws[5])))
            for c in some:
                u, left, right = beside(lambda cols: src[c, s + 1, here, cols], k)
                total = pushed(c, lanes)
                total = total + ws[0] * src[c, s + 2, here, lanes]
                total = total + ws[1] * src[c, s, here, lanes]
                total = total + ws[2] * src[c, s + 1, next_row, lanes]
                total = total + ws[3] * src[c, s + 1, last_row, lanes]
                total = total + ws[4] * left
                total = total + ws[5] * right
                store(c, lanes, 0.2 * u + rate * total)

    def sweep1(s, r, some):
        def store(c, lanes, value):
            u1[c, s + 1, PAD + r:PAD + r + 8, lanes] = value

        sweep(u0, s, PAD + r, 8, some, lambda c, lanes: fv[c, s, r:r + 8, lanes], store)

    def sweep2(s, r, some):
        def store(c, lanes, value):
            out[c, s, r:r + 8, lanes] = value

        sweep(u1, s, PAD + r, 8, some, lambda c, lanes: fv[c, s, r:r + 8, lanes], store)

    edge_rows = sorted({0, rows - 8})
    inner_rows = list(range(8, rows - 8, 8))
    all_comps, rest_comps = list(range(comps)), list(range(1, comps))

    def inner1(i, carry):
        s = order(i)
        for r in inner_rows:
            sweep1(s, r, all_comps)
        return carry

    lax.fori_loop(0, jnp.where(top, 2, 3), inner1, 0)

    quarter = lon // 4
    modes = th.shape[1] // 2
    wave = lax.broadcasted_iota(jnp.int32, (rows, modes), 1) & 3
    zero, one = jnp.zeros((rows, modes), f32), jnp.ones((rows, modes), f32)
    e1 = jnp.where(wave == 0, one, jnp.where(wave == 2, -one, zero))
    s1 = jnp.where(wave == 1, one, jnp.where(wave == 3, -one, zero))
    e2 = jnp.where((wave & 1) == 0, one, -one)
    half = width // rad
    forward = []
    for d, e in [(d, e) for d in range(lat) for e in range(rad) if d or e != rad - 1]:
        peer = lax.rem(me + d, lat)
        forward.append((d, e, pltpu.make_async_remote_copy(
            src_ref=fsend.at[peer, e], dst_ref=frecv.at[me],
            send_sem=a_send.at[d * rad + e], recv_sem=a_recv.at[d],
            device_id={"lateral": peer, "radial": e}, device_id_type=MESH)))

    @pl.when(top)
    def _():
        for side in sides:
            @pl.when(side[2])
            def _():
                for copy in first(side):
                    copy.wait_recv()
                lookup_at(shells, side[7])
                lookup_at(shells - 1, side[6])

        def early(i, carry):
            for r in edge_rows:
                sweep1(last - i, r, [0])
            return carry

        lax.fori_loop(0, 2, early, 0)
        for side, row in zip(sides, (PAD - 1, PAD + rows)):
            @pl.when(side[2])
            def _():
                def store(c, lanes, value):
                    u1[c, shells, row:row + 1, lanes] = value

                sweep(u0, last, row, 1, [0], lambda c, lanes: fh[side[0], :, lanes], store)

        for r in range(0, rows, 8):
            sweep2(last, r, [0])

    for copy in c_tables[:2]:
        copy.wait()

    @pl.when(top)
    def _():
        x = jnp.concatenate([out[0, last, :, quarter * m:quarter * (m + 1)] for m in range(4)], axis=0)
        xh, xl = split(x)
        g = dot(xh, th_v[...]) + dot(xl, th_v[...]) + dot(xh, tl_v[...])
        gc = [g[rows * m:rows * (m + 1), :modes] for m in range(4)]
        gs = [g[rows * m:rows * (m + 1), modes:] for m in range(4)]
        fc = gc[0] + e2 * gc[2] + e1 * (gc[1] + gc[3]) - s1 * (gs[1] - gs[3])
        fs = gs[0] + e2 * gs[2] + e1 * (gs[1] + gs[3]) + s1 * (gc[1] - gc[3])
        fourier = jnp.concatenate([fc, fs], axis=1)
        for p in range(lat):
            for e in range(rad):
                fsend[p, e] = fourier[:, p * width + e * half:p * width + (e + 1) * half]

    for k, step in enumerate(steps):
        if k > 1:
            pl.semaphore_wait(far_sem.at[k - 1], greeted(steps[k - 1]))
            greet(far_sem.at[k], step)
    pl.semaphore_wait(far_sem.at[len(steps) - 1], greeted(steps[-1]))

    @pl.when(top)
    def _():
        for _, _, copy in forward:
            copy.start()
        frecv[me] = fsend[me, rad - 1]

    def main(i, carry):
        s = order(i)

        @pl.when(i == last)
        def _():
            r_layer.wait_recv()
            r_disp.wait_recv()
            lookup(facing)

        @pl.when(jnp.logical_or(jnp.logical_and(top, i == 2), i == last))
        def _():
            inner1(i, 0)

        got_from(i, *bulk)
        for side in sides:
            @pl.when(jnp.logical_and(side[2], jnp.logical_not(jnp.logical_and(top, i < 2))))
            def _():
                lookup_at(s + 1, side[6])

        for r in edge_rows:
            sweep1(s, r, all_comps)
        start_to(i, *later)
        return carry

    lax.fori_loop(0, shells, main, 0)
    r_later.start()

    def inner2(i, carry):
        s = order(i)
        alone = jnp.logical_and(top, i == 0)

        @pl.when(alone)
        def _():
            for r in inner_rows:
                sweep2(s, r, rest_comps)

        @pl.when(jnp.logical_not(alone))
        def _():
            for r in inner_rows:
                sweep2(s, r, all_comps)

        return carry

    lax.fori_loop(0, last, inner2, 0)

    for copy in c_tables[2:]:
        copy.wait()
    answer = resp_v[:, :half]
    for e in range(1, rad):
        answer = jnp.where(place == e, resp_v[:, e * half:(e + 1) * half], answer)
    resp_t[...] = answer.T

    @pl.when(top)
    def _():
        for d, e, copy in forward:
            if e == rad - 1:
                copy.wait_recv()

    @pl.when(jnp.logical_not(top))
    def _():
        for d, e, copy in forward:
            if e == 0:
                copy.wait_recv()

    spectrum = frecv[...].reshape(lat * rows, half)
    sh, sl = split(spectrum)
    down = (((0,), (0,)), ((), ()))
    both = dot(jnp.concatenate([sh, sl], axis=1), ch_v[...], down)
    coef = both[:half] + both[half:] + dot(sh, cl_v[...], down)
    sh, sl = split(resp_t[...] * coef)
    nt = (((1,), (1,)), ((), ()))
    load_rows = dot(ch_v[...], sh, nt) + dot(ch_v[...], sl, nt) + dot(cl_v[...], sh, nt)
    gsend[...] = load_rows.reshape(lat, rows, half)
    back = []
    for d, e in offsets:
        back.append(pltpu.make_async_remote_copy(
            src_ref=gsend.at[lax.rem(me + d, lat)], dst_ref=grecv.at[me, place],
            send_sem=b_send.at[d * rad + e], recv_sem=b_recv.at[d * rad + e],
            device_id=around(d, e), device_id_type=MESH))
    for copy in back:
        copy.start()
    grecv[me, place] = gsend[me]
    coef_out[...] = coef

    def final(i, carry):
        s = order(i)
        alone = jnp.logical_and(top, i == 0)

        @pl.when(i == last)
        def _():
            r_later.wait_recv()
            inner2(i, 0)

        got_from(i, *later)

        @pl.when(alone)
        def _():
            for r in edge_rows:
                sweep2(s, r, rest_comps)

        @pl.when(jnp.logical_not(alone))
        def _():
            for r in edge_rows:
                sweep2(s, r, all_comps)

        return carry

    lax.fori_loop(0, shells, final, 0)

    @pl.when(top)
    def _():
        for _, _, copy in forward:
            copy.wait_send()
        for side in sides:
            @pl.when(side[1])
            def _():
                for copy in first(side):
                    copy.wait_send()

    def settle(i, carry):
        sent_to(i, *bulk)
        sent_to(i, *later)
        return carry

    lax.fori_loop(0, shells, settle, 0)
    for copy in (r_layer, r_disp, r_later):
        copy.wait_send()
    for copy in back:
        copy.wait()
    for p in range(lat):
        for e in range(rad):
            gather[:, p * width + e * half:p * width + (e + 1) * half] = grecv[p, e]


def finish(out, coef, gather, th, tl, mask, out_h, coef_h, sea_h, sea, sem):
    rows, lon = mask.shape
    quarter, modes = lon // 4, th.shape[1] // 2
    copies = [pltpu.make_async_copy(out, out_h, sem.at[0]), pltpu.make_async_copy(coef, coef_h, sem.at[1])]
    for copy in copies:
        copy.start()
    wave = lax.broadcasted_iota(jnp.int32, (rows, modes), 1) & 3
    zero, one = jnp.zeros((rows, modes), f32), jnp.ones((rows, modes), f32)
    e1 = jnp.where(wave == 0, one, jnp.where(wave == 2, -one, zero))
    s1 = jnp.where(wave == 1, one, jnp.where(wave == 3, -one, zero))
    e2 = jnp.where((wave & 1) == 0, one, -one)
    rc, rs = gather[:, :modes], gather[:, modes:]
    twisted = [
        (rc, rs),
        (e1 * rc + s1 * rs, e1 * rs - s1 * rc),
        (e2 * rc, e2 * rs),
        (e1 * rc - s1 * rs, e1 * rs + s1 * rc),
    ]
    a = jnp.concatenate([jnp.concatenate(pair, axis=1) for pair in twisted], axis=0)
    ah, al = split(a)
    nt = (((1,), (1,)), ((), ()))
    total = dot(ah, th[...], nt) + dot(al, th[...], nt) + dot(ah, tl[...], nt)
    for m in range(4):
        cut = slice(quarter * m, quarter * (m + 1))
        sea[:, cut] = mask[:, cut].astype(f32) * total[rows * m:rows * (m + 1)]
        copies.append(pltpu.make_async_copy(sea.at[:, cut], sea_h.at[:, cut], sem.at[2 + m]))
        copies[-1].start()
    for copy in copies:
        copy.wait()


def shards(lat, rad, disp, force, visc, layer, response, mask):
    comps, shells, rows, lon = disp.shape
    width = response.shape[1]
    th, tl = longitude_quarter(lon, MODES)
    ch, cl = colatitude_table(lat * rows, MODES)
    tables = [th, tl, ch, cl]
    hbm = pl.BlockSpec(memory_space=pltpu.HBM)
    vmem = pl.BlockSpec(memory_space=pltpu.VMEM)
    tall = rows + 2 * PAD
    field = pltpu.VMEM((comps, shells + 2, tall, lon), f32)
    half = width // rad
    block = pltpu.VMEM((lat, rows, half), f32)
    dma = pltpu.SemaphoreType.DMA
    spare = 4 * (disp.size + MODES * width // rad + 2 * rows * MODES + rows * lon) + 2 * (th.size + tl.size) + 65536
    kinds = 5 + 3 * shells
    out, coef, gather, th_v, tl_v, mask_v = pl.pallas_call(
        functools.partial(kernel, lat, rad, visc.shape[0]),
        out_shape=(
            pltpu.VMEM(disp.shape, f32),
            pltpu.VMEM((width // rad, MODES), f32),
            pltpu.VMEM((rows, 2 * MODES), f32),
            pltpu.VMEM(th.shape, bf16),
            pltpu.VMEM(tl.shape, bf16),
            pltpu.VMEM(mask.shape, jnp.int32),
        ),
        in_specs=[hbm] * 10,
        out_specs=(vmem,) * 6,
        scratch_shapes=[
            field, field,
            pltpu.VMEM((comps, shells, rows, lon), f32),
            pltpu.VMEM((2, 1, lon), f32),
            pltpu.VMEM((shells + 2, tall, lon), jnp.int32),
            pltpu.VMEM((shells + 2, tall, lon), f32),
            pltpu.VMEM((lat, rad, rows, half), f32), block, block, pltpu.VMEM((lat, rad, rows, half), f32),
            pltpu.VMEM(response.shape, f32), pltpu.VMEM((half, MODES), f32),
        ] + [pltpu.VMEM(t.shape, bf16) for t in tables[2:]] + [
            pltpu.SMEM(visc.shape, f32),
            dma((2 + 2 * comps + 6,)), dma((2, kinds)), dma((2, kinds)), dma((3,)), dma((3,)),
            dma((lat * rad,)), dma((lat,)), dma((lat * rad,)), dma((lat * rad,)),
            pltpu.SemaphoreType.REGULAR((max(1, (lat - 1).bit_length()),)),
        ],
        compiler_params=pltpu.CompilerParams(
            collective_id=0, has_side_effects=True, vmem_limit_bytes=VMEM - spare),
    )(disp, force, visc, layer, response, mask, *[jnp.asarray(t) for t in tables])
    out, coef, sea = pl.pallas_call(
        finish,
        out_shape=tuple(jax.ShapeDtypeStruct(shape, f32) for shape in (out.shape, coef.shape, mask.shape)),
        in_specs=[vmem] * 6,
        out_specs=(hbm, hbm, hbm),
        scratch_shapes=[pltpu.VMEM(mask.shape, f32), dma((6,))],
        compiler_params=pltpu.CompilerParams(vmem_limit_bytes=8 << 20),
    )(out, coef, gather, th_v, tl_v, mask_v)
    return out, coef.T, sea


def solution(mesh):
    in_specs = (
        P("member", "radial", "lateral", None),
        P("member", "radial", "lateral", None),
        P("member"),
        P("radial", "lateral", None),
        P(None, "lateral"),
        P("lateral", None),
    )
    out_specs = (
        P("member", "radial", "lateral", None),
        P("member", ("lateral", "radial")),
        P("lateral", "member"),
    )
    body = functools.partial(shards, mesh.shape["lateral"], mesh.shape["radial"])
    return jax.shard_map(body, mesh=mesh, in_specs=in_specs, out_specs=out_specs, check_vma=False)
```

profile of v0, /device:TPU:1, one launch (start us, length us, event | category | flops | bytes accessed | tf_op | source)
XLA Modules:
  0.0 28.6 jit_solution(9883230989514149411)
XLA Ops:
  0.6 26.1 %shard_map.121 = (f32[3,4,32,2048]{3,2,1,0:T(8,128)S(1)}, f32[64,512]{1,0:T(8,128)S(1)}, f32[32,1024]{1,0:T(8,128)S(1)}, bf16[512,1024]{1,0:T(8,128)(2,1)S(1)}, ...) custom-call(f32[3,4,32,2048]{3,2,1,0:T(8,128)} %disp.1, f32[3,4,32,2048]{3,2,1,0:T(8,128)} %force.1, f32[16]{0:T(128)} %visc.1, ...), custom_call_target="tpu_custom_call" | custom-call | tf_op jit(solution)/shard_map/pallas_call | solution.py:589
  26.7 1.9 %shard_map.122 = (f32[3,4,32,2048]{3,2,1,0:T(8,128)}, f32[64,512]{1,0:T(8,128)}, f32[32,2048]{1,0:T(8,128)}) custom-call(f32[3,4,32,2048]{3,2,1,0:T(8,128)S(1)} %get-tuple-element.12.out, f32[64,512]{1,0:T(8,128)S(1)} %get-tuple-element.13.coef, f32[32,1024]{1,0:T(8,128)S(1)} %get-tuple-element.14.gather, bf16[512,1024]{1,0:T(8,128)(2,1)S(1)} %get-tuple-element.15.th, ...), custom_call_target="tpu_custom_call" | custom-call | tf_op jit(solution)/shard_map/pallas_call | solution.py:618
where the time goes:
time: 28.7 us; the launch traced here: 28.6 us
  Pallas kernels  27.9 us (97%)
  between operations  0.64 us (2%)
    pallas_call x1, Pallas kernels, shards(): pl.pallas_call(functools.partial(kernel, lat, rad, visc.shape[0]), out_sh...  26.1 us
    pallas_call x1, Pallas kernels, shards(): pl.pallas_call(finish, out_shape=tuple((jax.ShapeDtypeStruct(shape, f32)...  1.88 us

commit v1 on v0

--- a/solution.py
+++ b/solution.py
@@ -190,11 +190,31 @@
         def _():
             act(every)
 
+    odd = lax.rem(me, 2) == 1
+
+    def nearer_first(go):
+        @pl.when(odd)
+        def _():
+            go(sides[1])
+
+        go(sides[0])
+
+        @pl.when(jnp.logical_not(odd))
+        def _():
+            go(sides[1])
+
     def start_to(i, some, every):
         for side in sides:
             @pl.when(side[1])
             def _():
                 for_shell(i, lambda make: [c.start() for c in make(side, i)], some, every)
+
+    def start_bulk(near):
+        for side in sides:
+            @pl.when(jnp.logical_and(side[1], odd == ((side[0] == 1) == near)))
+            def _():
+                for i in range(shells):
+                    for_shell(i, lambda make: [c.start() for c in make(side, i)], *bulk)
 
     def sent_to(i, some, every):
         for side in sides:
@@ -226,21 +246,18 @@
 
     @pl.when(top)
     def _():
-        for side in sides:
+        def go(side):
             @pl.when(side[1])
             def _():
                 for copy in first(side):
                     copy.start()
+
+        nearer_first(go)
 
     r_layer.start()
     r_disp.start()
     greet(far_sem.at[0], steps[0])
 
-    @pl.when(top)
-    def _():
-        for i in range(shells):
-            start_to(i, *bulk)
-
     c_visc.wait()
     values = [visc_s[i] * 0.5 for i in range(layers)]
 
@@ -258,21 +275,16 @@
     c_layer.wait()
     lax.fori_loop(0, shells, lookup_step, 0)
 
-    @pl.when(jnp.logical_not(top))
-    def _():
-        for i in range(shells):
-            start_to(i, *bulk)
+    start_bulk(True)
 
     tables = [(th, th_v), (tl, tl_v), (response, resp_v), (ch, ch_v), (cl, cl_v), (mask, mask_v)]
     for copy in c_disp + c_force:
         copy.wait()
     c_tables = [load(a, b, 2 + 2 * comps + k) for k, (a, b) in enumerate(tables)]
 
-    for k, step in enumerate(steps):
-        if k:
-            pl.semaphore_wait(far_sem.at[k - 1], greeted(steps[k - 1]))
-            greet(far_sem.at[k], step)
-            break
+    if steps[1:]:
+        pl.semaphore_wait(far_sem.at[0], greeted(steps[0]))
+        greet(far_sem.at[1], steps[1])
 
     chunk = lon // 4
 
@@ -333,6 +345,12 @@
         return carry
 
     lax.fori_loop(0, jnp.where(top, 2, 3), inner1, 0)
+    start_bulk(False)
+
+    for k, step in enumerate(steps):
+        if k > 1:
+            pl.semaphore_wait(far_sem.at[k - 1], greeted(steps[k - 1]))
+            greet(far_sem.at[k], step)
 
     quarter = lon // 4
     modes = th.shape[1] // 2
@@ -394,10 +412,6 @@
             for e in range(rad):
                 fsend[p, e] = fourier[:, p * width + e * half:p * width + (e + 1) * half]
 
-    for k, step in enumerate(steps):
-        if k > 1:
-            pl.semaphore_wait(far_sem.at[k - 1], greeted(steps[k - 1]))
-            greet(far_sem.at[k], step)
     pl.semaphore_wait(far_sem.at[len(steps) - 1], greeted(steps[-1]))
 
     @pl.when(top)
@@ -448,8 +462,6 @@
                 sweep2(s, r, all_comps)
 
         return carry
-
-    lax.fori_loop(0, last, inner2, 0)
 
     for copy in c_tables[2:]:
         copy.wait()
@@ -512,6 +524,8 @@
                 sweep2(s, r, all_comps)
 
         return carry
+
+    lax.fori_loop(0, last, inner2, 0)
 
     lax.fori_loop(0, shells, final, 0)
 

time: 28.7 us -> 25.4 us (0.89)
  the two profiles are of different devices: /device:TPU:1 before, /device:TPU:0 now
where the time goes in v1:
time: 25.4 us; the launch traced here: 25.3 us
  Pallas kernels  24.6 us (97%)
  between operations  0.64 us (3%)
    pallas_call x1, Pallas kernels, shards(): pl.pallas_call(functools.partial(kernel, lat, rad, visc.shape[0]), out_sh...  22.7 us
    pallas_call x1, Pallas kernels, shards(): pl.pallas_call(finish, out_shape=tuple((jax.ShapeDtypeStruct(shape, f32)...  1.87 us

profile of v1, /device:TPU:0, one launch (start us, length us, event | category | flops | bytes accessed | tf_op | source)
XLA Modules:
  0.0 25.3 jit_solution(15737617090821371500)
XLA Ops:
  0.6 22.7 %shard_map.121 = (f32[3,4,32,2048]{3,2,1,0:T(8,128)S(1)}, f32[64,512]{1,0:T(8,128)S(1)}, f32[32,1024]{1,0:T(8,128)S(1)}, bf16[512,1024]{1,0:T(8,128)(2,1)S(1)}, ...) custom-call(f32[3,4,32,2048]{3,2,1,0:T(8,128)} %disp.1, f32[3,4,32,2048]{3,2,1,0:T(8,128)} %force.1, f32[16]{0:T(128)} %visc.1, ...), custom_call_target="tpu_custom_call" | custom-call | tf_op jit(solution)/shard_map/pallas_call | solution.py:603
  23.4 1.9 %shard_map.122 = (f32[3,4,32,2048]{3,2,1,0:T(8,128)}, f32[64,512]{1,0:T(8,128)}, f32[32,2048]{1,0:T(8,128)}) custom-call(f32[3,4,32,2048]{3,2,1,0:T(8,128)S(1)} %get-tuple-element.12.out, f32[64,512]{1,0:T(8,128)S(1)} %get-tuple-element.13.coef, f32[32,1024]{1,0:T(8,128)S(1)} %get-tuple-element.14.gather, bf16[512,1024]{1,0:T(8,128)(2,1)S(1)} %get-tuple-element.15.th, ...), custom_call_target="tpu_custom_call" | custom-call | tf_op jit(solution)/shard_map/pallas_call | solution.py:632

commit v2 on v1

--- a/solution.py
+++ b/solution.py
@@ -60,10 +60,10 @@
     return values[0]
 
 
-def kernel(lat, rad, layers, disp, force, visc, layer, response, mask, th, tl, ch, cl,
-           out, coef_out, gather, th_v, tl_v, mask_v,
-           u0, u1, fv, fh, li, he, fsend, frecv, gsend, grecv, resp_v, resp_t, ch_v, cl_v, visc_s,
-           load_sem, x_send, x_recv, r_send, r_recv, a_send, a_recv, b_send, b_recv, far_sem):
+def kernel(lat, rad, layers, disp, force, visc, layer, response, mask, trig, cosine,
+           out, coef_out, gather, trig_v, mask_v,
+           u0, u1, fv, fh, li, he, fsend, frecv, gsend, grecv, resp_v, resp_t, cosine_v, visc_s,
+           load_sem, send_sem, x_recv, r_recv, all_recv, far_sem):
     comps, shells, rows, lon = disp.shape
     width = response.shape[1]
     me = lax.axis_index("lateral")
@@ -82,13 +82,16 @@
         copy.start()
         return copy
 
-    def field(c):
-        return u0.at[c, pl.ds(1, shells), inner]
+    def arrived(ref, sem):
+        pltpu.make_async_copy(ref, ref, sem).wait()
+
+    def peer(d):
+        return me ^ d if lat & (lat - 1) == 0 else lax.rem(me + d, lat)
 
     def around(d, e):
-        return {"lateral": lax.rem(me + d, lat), "radial": lax.rem(place + e, rad)}
-
-    offsets = [(d, e) for d in range(lat) for e in range(rad) if d or e]
+        return {"lateral": peer(d), "radial": lax.rem(place + e, rad)}
+
+    offsets = [(d, e) for d in reversed(range(lat)) for e in range(rad) if d or e]
     barrier = pltpu.get_barrier_semaphore()
     for e in range(1, rad):
         pl.semaphore_signal(barrier, inc=1, device_id=around(0, e), device_id_type=MESH)
@@ -110,10 +113,8 @@
 
     c_visc = load(visc, visc_s, 0)
     c_layer = load(layer, li.at[pl.ds(1, shells), inner], 1)
-    c_disp, c_force = [], []
-    for c in range(comps):
-        c_disp.append(load(disp.at[c], field(c), 2 + 2 * c))
-        c_force.append(load(force.at[c], fv.at[c], 3 + 2 * c))
+    c_disp = load(disp, u0.at[:, pl.ds(1, shells), inner], 2)
+    c_force = load(force, fv, 3)
 
     void = jnp.where(top, shells + 1, 0)
     tall, wide = rows + 2 * PAD, (1, lon)
@@ -146,7 +147,7 @@
 
     def lateral(side, k, source, target):
         return pltpu.make_async_remote_copy(
-            src_ref=source, dst_ref=target, send_sem=x_send.at[side[0], k], recv_sem=x_recv.at[side[0], k],
+            src_ref=source, dst_ref=target, send_sem=send_sem.at[side[0]], recv_sem=x_recv.at[side[0], k],
             device_id={"lateral": side[3]}, device_id_type=MESH)
 
     def first(side):
@@ -158,26 +159,26 @@
             (layer.at[last - 1, one], li.at[shells - 1, edge]),
             (force.at[0, last, one], fh.at[side[0]]),
         ]
-        return [lateral(side, k, a, b) for k, (a, b) in enumerate(refs)]
+        return [lateral(side, 0, a, b) for a, b in refs]
 
     rest = pl.ds(1, comps - 1)
 
     def bulk_rest(side, i):
         s = order(i)
-        return [lateral(side, 5 + i, disp.at[rest, s, side[4]], u0.at[rest, s + 1, side[6]])]
+        return [lateral(side, 1 + i, disp.at[rest, s, side[4]], u0.at[rest, s + 1, side[6]])]
 
     def bulk_all(side, i):
         s = order(i)
-        return [lateral(side, 5 + shells + i, layer.at[s, side[4]], li.at[s + 1, side[6]]),
-                lateral(side, 5 + i, disp.at[:, s, side[4]], u0.at[:, s + 1, side[6]])]
+        return [lateral(side, 1 + i, layer.at[s, side[4]], li.at[s + 1, side[6]]),
+                lateral(side, 1 + i, disp.at[:, s, side[4]], u0.at[:, s + 1, side[6]])]
 
     def later_rest(side, i):
         s = order(i)
-        return [lateral(side, 5 + 2 * shells + i, u1.at[rest, s + 1, side[8]], u1.at[rest, s + 1, side[6]])]
+        return [lateral(side, 1 + shells + i, u1.at[rest, s + 1, side[8]], u1.at[rest, s + 1, side[6]])]
 
     def later_all(side, i):
         s = order(i)
-        return [lateral(side, 5 + 2 * shells + i, u1.at[:, s + 1, side[8]], u1.at[:, s + 1, side[6]])]
+        return [lateral(side, 1 + shells + i, u1.at[:, s + 1, side[8]], u1.at[:, s + 1, side[6]])]
 
     def for_shell(i, act, some, every):
         alone = jnp.logical_and(top, i < some[1])
@@ -188,7 +189,7 @@
 
         @pl.when(jnp.logical_not(alone))
         def _():
-            act(every)
+            act(every[0])
 
     odd = lax.rem(me, 2) == 1
 
@@ -204,43 +205,46 @@
             go(sides[1])
 
     def start_to(i, some, every):
+        def go(side):
+            @pl.when(side[1])
+            def _():
+                for_shell(i, lambda make: [c.start() for c in make(side, i)], some, every)
+
+        nearer_first(go)
+
+    def got_from(i, k, some, every):
         for side in sides:
-            @pl.when(side[1])
-            def _():
-                for_shell(i, lambda make: [c.start() for c in make(side, i)], some, every)
-
-    def start_bulk(near):
-        for side in sides:
-            @pl.when(jnp.logical_and(side[1], odd == ((side[0] == 1) == near)))
-            def _():
-                for i in range(shells):
-                    for_shell(i, lambda make: [c.start() for c in make(side, i)], *bulk)
-
-    def sent_to(i, some, every):
-        for side in sides:
-            @pl.when(side[1])
-            def _():
-                for_shell(i, lambda make: [c.wait_send() for c in make(side, i)], some, every)
-
-    def got_from(i, some, every):
-        for side in sides:
-            @pl.when(side[2])
-            def _():
-                for_shell(i, lambda make: [c.wait_recv() for c in make(side, i)], some, every)
-
-    bulk = ((bulk_rest, 2), bulk_all)
-    later = ((later_rest, 1), later_all)
+            alone = jnp.logical_and(top, i < some[1])
+            sem = x_recv.at[side[0], k + i]
+
+            @pl.when(jnp.logical_and(side[2], alone))
+            def _():
+                arrived(span(some[2]), sem)
+
+            @pl.when(jnp.logical_and(side[2], jnp.logical_not(alone)))
+            def _():
+                arrived(span(every[1]), sem)
+
+    def span(count):
+        parts = min(n for n in range(1, shells + 3) if count % n == 0 and count // n <= 8)
+        return u0.at[0, pl.ds(0, parts), pl.ds(0, 8), pl.ds(0, count // parts * (lon // 8))]
+
+    bulk = ((bulk_rest, 2, comps - 1), (bulk_all, comps + 1))
+    later = ((later_rest, 1, comps - 1), (later_all, comps))
+    rows_first = 7
+    rows_top = rows_first + sum(k[0][1] * k[0][2] + (shells - k[0][1]) * k[1][1] for k in (bulk, later))
+    rows_other = sum(shells * k[1][1] for k in (bulk, later))
 
     def across(k, source, target):
         return pltpu.make_async_remote_copy(
-            src_ref=source, dst_ref=target, send_sem=r_send.at[k], recv_sem=r_recv.at[k],
+            src_ref=source, dst_ref=target, send_sem=send_sem.at[2 + k], recv_sem=r_recv.at[k],
             device_id={"radial": rad - 1 - place}, device_id_type=MESH)
 
     beyond = jnp.where(top, shells + 1, 0)
     facing = jnp.where(top, 0, shells + 1)
     r_layer = across(0, layer.at[face], li.at[beyond, inner])
-    r_disp = across(1, disp.at[:, face], u0.at[:, beyond, inner])
-    r_later = across(2, u1.at[:, face + 1, inner], u1.at[:, beyond, inner])
+    r_disp = across(0, disp.at[:, face], u0.at[:, beyond, inner])
+    r_later = across(1, u1.at[:, face + 1, inner], u1.at[:, beyond, inner])
 
     pl.semaphore_wait(barrier, greeted(1) + rad - 1)
 
@@ -275,16 +279,18 @@
     c_layer.wait()
     lax.fori_loop(0, shells, lookup_step, 0)
 
-    start_bulk(True)
-
-    tables = [(th, th_v), (tl, tl_v), (response, resp_v), (ch, ch_v), (cl, cl_v), (mask, mask_v)]
-    for copy in c_disp + c_force:
-        copy.wait()
-    c_tables = [load(a, b, 2 + 2 * comps + k) for k, (a, b) in enumerate(tables)]
-
+    start_to(0, *bulk)
     if steps[1:]:
         pl.semaphore_wait(far_sem.at[0], greeted(steps[0]))
         greet(far_sem.at[1], steps[1])
+
+    c_disp.wait()
+    c_force.wait()
+    start_to(1, *bulk)
+    tables = [(trig, trig_v), (response, resp_v), (cosine, cosine_v), (mask, mask_v)]
+    c_tables = [load(a, b, 4 + k) for k, (a, b) in enumerate(tables)]
+
+    start_to(2, *bulk)
 
     chunk = lon // 4
 
@@ -345,15 +351,13 @@
         return carry
 
     lax.fori_loop(0, jnp.where(top, 2, 3), inner1, 0)
-    start_bulk(False)
-
     for k, step in enumerate(steps):
         if k > 1:
             pl.semaphore_wait(far_sem.at[k - 1], greeted(steps[k - 1]))
             greet(far_sem.at[k], step)
 
     quarter = lon // 4
-    modes = th.shape[1] // 2
+    modes = trig.shape[2] // 2
     wave = lax.broadcasted_iota(jnp.int32, (rows, modes), 1) & 3
     zero, one = jnp.zeros((rows, modes), f32), jnp.ones((rows, modes), f32)
     e1 = jnp.where(wave == 0, one, jnp.where(wave == 2, -one, zero))
@@ -361,20 +365,18 @@
     e2 = jnp.where((wave & 1) == 0, one, -one)
     half = width // rad
     forward = []
-    for d, e in [(d, e) for d in range(lat) for e in range(rad) if d or e != rad - 1]:
-        peer = lax.rem(me + d, lat)
+    for d, e in [(d, e) for d in reversed(range(lat)) for e in range(rad) if d or e != rad - 1]:
         forward.append((d, e, pltpu.make_async_remote_copy(
-            src_ref=fsend.at[peer, e], dst_ref=frecv.at[me],
-            send_sem=a_send.at[d * rad + e], recv_sem=a_recv.at[d],
-            device_id={"lateral": peer, "radial": e}, device_id_type=MESH)))
+            src_ref=fsend.at[peer(d) * rad + e], dst_ref=frecv.at[me],
+            send_sem=send_sem.at[4], recv_sem=all_recv.at[0],
+            device_id={"lateral": peer(d), "radial": e}, device_id_type=MESH)))
 
     @pl.when(top)
     def _():
         for side in sides:
             @pl.when(side[2])
             def _():
-                for copy in first(side):
-                    copy.wait_recv()
+                arrived(span(rows_first), x_recv.at[side[0], 0])
                 lookup_at(shells, side[7])
                 lookup_at(shells - 1, side[6])
 
@@ -395,14 +397,13 @@
         for r in range(0, rows, 8):
             sweep2(last, r, [0])
 
-    for copy in c_tables[:2]:
-        copy.wait()
+    c_tables[0].wait()
 
     @pl.when(top)
     def _():
         x = jnp.concatenate([out[0, last, :, quarter * m:quarter * (m + 1)] for m in range(4)], axis=0)
         xh, xl = split(x)
-        g = dot(xh, th_v[...]) + dot(xl, th_v[...]) + dot(xh, tl_v[...])
+        g = dot(xh, trig_v[0]) + dot(xl, trig_v[0]) + dot(xh, trig_v[1])
         gc = [g[rows * m:rows * (m + 1), :modes] for m in range(4)]
         gs = [g[rows * m:rows * (m + 1), modes:] for m in range(4)]
         fc = gc[0] + e2 * gc[2] + e1 * (gc[1] + gc[3]) - s1 * (gs[1] - gs[3])
@@ -410,7 +411,7 @@
         fourier = jnp.concatenate([fc, fs], axis=1)
         for p in range(lat):
             for e in range(rad):
-                fsend[p, e] = fourier[:, p * width + e * half:p * width + (e + 1) * half]
+                fsend[p * rad + e] = fourier[:, p * width + e * half:p * width + (e + 1) * half]
 
     pl.semaphore_wait(far_sem.at[len(steps) - 1], greeted(steps[-1]))
 
@@ -418,22 +419,24 @@
     def _():
         for _, _, copy in forward:
             copy.start()
-        frecv[me] = fsend[me, rad - 1]
+        frecv[me] = fsend[me * rad + rad - 1]
+
+    for i in range(3, shells):
+        start_to(i, *bulk)
 
     def main(i, carry):
         s = order(i)
 
         @pl.when(i == last)
         def _():
-            r_layer.wait_recv()
-            r_disp.wait_recv()
+            arrived(u0.at[0, pl.ds(0, comps + 1), inner], r_recv.at[0])
             lookup(facing)
 
         @pl.when(jnp.logical_or(jnp.logical_and(top, i == 2), i == last))
         def _():
             inner1(i, 0)
 
-        got_from(i, *bulk)
+        got_from(i, 1, *bulk)
         for side in sides:
             @pl.when(jnp.logical_and(side[2], jnp.logical_not(jnp.logical_and(top, i < 2))))
             def _():
@@ -444,8 +447,7 @@
         start_to(i, *later)
         return carry
 
-    lax.fori_loop(0, shells, main, 0)
-    r_later.start()
+    lax.fori_loop(0, last, main, 0)
 
     def inner2(i, carry):
         s = order(i)
@@ -463,7 +465,7 @@
 
         return carry
 
-    for copy in c_tables[2:]:
+    for copy in c_tables[1:]:
         copy.wait()
     answer = resp_v[:, :half]
     for e in range(1, rad):
@@ -472,34 +474,30 @@
 
     @pl.when(top)
     def _():
-        for d, e, copy in forward:
-            if e == rad - 1:
-                copy.wait_recv()
+        arrived(frecv.at[pl.ds(0, lat - 1)], all_recv.at[0])
 
     @pl.when(jnp.logical_not(top))
     def _():
-        for d, e, copy in forward:
-            if e == 0:
-                copy.wait_recv()
+        arrived(frecv, all_recv.at[0])
 
     spectrum = frecv[...].reshape(lat * rows, half)
     sh, sl = split(spectrum)
     down = (((0,), (0,)), ((), ()))
-    both = dot(jnp.concatenate([sh, sl], axis=1), ch_v[...], down)
-    coef = both[:half] + both[half:] + dot(sh, cl_v[...], down)
+    both = dot(jnp.concatenate([sh, sl], axis=1), cosine_v[0], down)
+    coef = both[:half] + both[half:] + dot(sh, cosine_v[1], down)
     sh, sl = split(resp_t[...] * coef)
     nt = (((1,), (1,)), ((), ()))
-    load_rows = dot(ch_v[...], sh, nt) + dot(ch_v[...], sl, nt) + dot(cl_v[...], sh, nt)
+    load_rows = dot(cosine_v[0], sh, nt) + dot(cosine_v[0], sl, nt) + dot(cosine_v[1], sh, nt)
     gsend[...] = load_rows.reshape(lat, rows, half)
     back = []
     for d, e in offsets:
         back.append(pltpu.make_async_remote_copy(
-            src_ref=gsend.at[lax.rem(me + d, lat)], dst_ref=grecv.at[me, place],
-            send_sem=b_send.at[d * rad + e], recv_sem=b_recv.at[d * rad + e],
+            src_ref=gsend.at[peer(d)], dst_ref=grecv.at[me * rad + place],
+            send_sem=send_sem.at[5], recv_sem=all_recv.at[1],
             device_id=around(d, e), device_id_type=MESH))
     for copy in back:
         copy.start()
-    grecv[me, place] = gsend[me]
+    grecv[me * rad + place] = gsend[me]
     coef_out[...] = coef
 
     def final(i, carry):
@@ -511,7 +509,7 @@
             r_later.wait_recv()
             inner2(i, 0)
 
-        got_from(i, *later)
+        got_from(i, 1 + shells, *later)
 
         @pl.when(alone)
         def _():
@@ -525,38 +523,37 @@
 
         return carry
 
+    main(last, 0)
+    r_later.start()
+
     lax.fori_loop(0, last, inner2, 0)
 
     lax.fori_loop(0, shells, final, 0)
 
+    blocks = lat * rad - 1
+
     @pl.when(top)
     def _():
-        for _, _, copy in forward:
-            copy.wait_send()
-        for side in sides:
-            @pl.when(side[1])
-            def _():
-                for copy in first(side):
-                    copy.wait_send()
-
-    def settle(i, carry):
-        sent_to(i, *bulk)
-        sent_to(i, *later)
-        return carry
-
-    lax.fori_loop(0, shells, settle, 0)
-    for copy in (r_layer, r_disp, r_later):
-        copy.wait_send()
-    for copy in back:
-        copy.wait()
+        arrived(fsend.at[pl.ds(0, blocks)], send_sem.at[4])
+
+    for side in sides:
+        for who, count in ((top, rows_top), (jnp.logical_not(top), rows_other)):
+            @pl.when(jnp.logical_and(who, side[1]))
+            def _():
+                arrived(span(count), send_sem.at[side[0]])
+
+    arrived(u0.at[0, pl.ds(0, comps + 1), inner], send_sem.at[2])
+    arrived(u0.at[:, 0, inner], send_sem.at[3])
+    arrived(grecv.at[pl.ds(0, blocks)], send_sem.at[5])
+    arrived(grecv.at[pl.ds(0, blocks)], all_recv.at[1])
     for p in range(lat):
         for e in range(rad):
-            gather[:, p * width + e * half:p * width + (e + 1) * half] = grecv[p, e]
-
-
-def finish(out, coef, gather, th, tl, mask, out_h, coef_h, sea_h, sea, sem):
+            gather[:, p * width + e * half:p * width + (e + 1) * half] = grecv[p * rad + e]
+
+
+def finish(out, coef, gather, trig, mask, out_h, coef_h, sea_h, sea, sem):
     rows, lon = mask.shape
-    quarter, modes = lon // 4, th.shape[1] // 2
+    quarter, modes = lon // 4, trig.shape[2] // 2
     copies = [pltpu.make_async_copy(out, out_h, sem.at[0]), pltpu.make_async_copy(coef, coef_h, sem.at[1])]
     for copy in copies:
         copy.start()
@@ -575,7 +572,7 @@
     a = jnp.concatenate([jnp.concatenate(pair, axis=1) for pair in twisted], axis=0)
     ah, al = split(a)
     nt = (((1,), (1,)), ((), ()))
-    total = dot(ah, th[...], nt) + dot(al, th[...], nt) + dot(ah, tl[...], nt)
+    total = dot(ah, trig[0], nt) + dot(al, trig[0], nt) + dot(ah, trig[1], nt)
     for m in range(4):
         cut = slice(quarter * m, quarter * (m + 1))
         sea[:, cut] = mask[:, cut].astype(f32) * total[rows * m:rows * (m + 1)]
@@ -588,9 +585,9 @@
 def shards(lat, rad, disp, force, visc, layer, response, mask):
     comps, shells, rows, lon = disp.shape
     width = response.shape[1]
-    th, tl = longitude_quarter(lon, MODES)
-    ch, cl = colatitude_table(lat * rows, MODES)
-    tables = [th, tl, ch, cl]
+    trig = np.stack(longitude_quarter(lon, MODES))
+    cosine = np.stack(colatitude_table(lat * rows, MODES))
+    tables = [trig, cosine]
     hbm = pl.BlockSpec(memory_space=pltpu.HBM)
     vmem = pl.BlockSpec(memory_space=pltpu.VMEM)
     tall = rows + 2 * PAD
@@ -598,32 +595,29 @@
     half = width // rad
     block = pltpu.VMEM((lat, rows, half), f32)
     dma = pltpu.SemaphoreType.DMA
-    spare = 4 * (disp.size + MODES * width // rad + 2 * rows * MODES + rows * lon) + 2 * (th.size + tl.size) + 65536
-    kinds = 5 + 3 * shells
-    out, coef, gather, th_v, tl_v, mask_v = pl.pallas_call(
+    spare = 4 * (disp.size + MODES * width // rad + 2 * rows * MODES + rows * lon) + 2 * trig.size + 65536
+    out, coef, gather, trig_v, mask_v = pl.pallas_call(
         functools.partial(kernel, lat, rad, visc.shape[0]),
         out_shape=(
             pltpu.VMEM(disp.shape, f32),
             pltpu.VMEM((width // rad, MODES), f32),
             pltpu.VMEM((rows, 2 * MODES), f32),
-            pltpu.VMEM(th.shape, bf16),
-            pltpu.VMEM(tl.shape, bf16),
+            pltpu.VMEM(trig.shape, bf16),
             pltpu.VMEM(mask.shape, jnp.int32),
         ),
-        in_specs=[hbm] * 10,
-        out_specs=(vmem,) * 6,
+        in_specs=[hbm] * 8,
+        out_specs=(vmem,) * 5,
         scratch_shapes=[
             field, field,
             pltpu.VMEM((comps, shells, rows, lon), f32),
             pltpu.VMEM((2, 1, lon), f32),
             pltpu.VMEM((shells + 2, tall, lon), jnp.int32),
             pltpu.VMEM((shells + 2, tall, lon), f32),
-            pltpu.VMEM((lat, rad, rows, half), f32), block, block, pltpu.VMEM((lat, rad, rows, half), f32),
+            pltpu.VMEM((lat * rad, rows, half), f32), block, block, pltpu.VMEM((lat * rad, rows, half), f32),
             pltpu.VMEM(response.shape, f32), pltpu.VMEM((half, MODES), f32),
-        ] + [pltpu.VMEM(t.shape, bf16) for t in tables[2:]] + [
+            pltpu.VMEM(cosine.shape, bf16),
             pltpu.SMEM(visc.shape, f32),
-            dma((2 + 2 * comps + 6,)), dma((2, kinds)), dma((2, kinds)), dma((3,)), dma((3,)),
-            dma((lat * rad,)), dma((lat,)), dma((lat * rad,)), dma((lat * rad,)),
+            dma((8,)), dma((6,)), dma((2, 1 + 2 * shells)), dma((2,)), dma((2,)),
             pltpu.SemaphoreType.REGULAR((max(1, (lat - 1).bit_length()),)),
         ],
         compiler_params=pltpu.CompilerParams(
@@ -632,11 +626,11 @@
     out, coef, sea = pl.pallas_call(
         finish,
         out_shape=tuple(jax.ShapeDtypeStruct(shape, f32) for shape in (out.shape, coef.shape, mask.shape)),
-        in_specs=[vmem] * 6,
+        in_specs=[vmem] * 5,
         out_specs=(hbm, hbm, hbm),
         scratch_shapes=[pltpu.VMEM(mask.shape, f32), dma((6,))],
         compiler_params=pltpu.CompilerParams(vmem_limit_bytes=8 << 20),
-    )(out, coef, gather, th_v, tl_v, mask_v)
+    )(out, coef, gather, trig_v, mask_v)
     return out, coef.T, sea
 
 

time: 25.4 us -> 25.4 us (level)
  no operation moved by 1% of the time
where the time goes in v2:
time: 25.4 us; the launch traced here: 25.3 us
  Pallas kernels  24.7 us (97%)
  between operations  0.64 us (3%)
    pallas_call x1, Pallas kernels, shards(): pl.pallas_call(functools.partial(kernel, lat, rad, visc.shape[0]), out_sh...  22.8 us
    pallas_call x1, Pallas kernels, shards(): pl.pallas_call(finish, out_shape=tuple((jax.ShapeDtypeStruct(shape, f32)...  1.87 us

profile of v2, /device:TPU:0, one launch (start us, length us, event | category | flops | bytes accessed | tf_op | source)
XLA Modules:
  0.0 25.3 jit_solution(14379503207650997878)
XLA Ops:
  0.6 22.8 %shard_map.103 = (f32[3,4,32,2048]{3,2,1,0:T(8,128)S(1)}, f32[64,512]{1,0:T(8,128)S(1)}, f32[32,1024]{1,0:T(8,128)S(1)}, bf16[2,512,1024]{2,1,0:T(8,128)(2,1)S(1)}, s32[32,2048]{1,0:T(8,128)S(1)}) custom-call(f32[3,4,32,2048]{3,2,1,0:T(8,128)} %disp.1, f32[3,4,32,2048]{3,2,1,0:T(8,128)} %force.1, f32[16]{0:T(128)} %visc.1, s32[4,32,2048]{2,1,0:T(8,128)} %layer.1, ...), custom_call_target="tpu_custom_call" | custom-call | tf_op jit(solution)/shard_map/pallas_call | solution.py:599
  23.4 1.9 %shard_map.104 = (f32[3,4,32,2048]{3,2,1,0:T(8,128)}, f32[64,512]{1,0:T(8,128)}, f32[32,2048]{1,0:T(8,128)}) custom-call(f32[3,4,32,2048]{3,2,1,0:T(8,128)S(1)} %get-tuple-element.11.out, f32[64,512]{1,0:T(8,128)S(1)} %get-tuple-element.12.coef, f32[32,1024]{1,0:T(8,128)S(1)} %get-tuple-element.13.gather, bf16[2,512,1024]{2,1,0:T(8,128)(2,1)S(1)} %get-tuple-element.14.trig, ...), custom_call_target="tpu_custom_call" | custom-call | tf_op jit(solution)/shard_map/pallas_call | solution.py:626

commit v3 on v2

--- a/solution.py
+++ b/solution.py
@@ -46,6 +46,12 @@
 
 def dot(a, b, dims=(((1,), (0,)), ((), ()))):
     return lax.dot_general(a, b, dims, preferred_element_type=f32)
+
+
+def swap(a, b):
+    half = a.shape[-1] // 2
+    low = lax.broadcasted_iota(jnp.int32, a.shape, a.ndim - 1) < half
+    return jnp.where(low, a, pltpu.roll(b, half, a.ndim - 1)), jnp.where(low, pltpu.roll(a, half, a.ndim - 1), b)
 
 
 def choose(index, values):
@@ -350,7 +356,8 @@
             sweep1(s, r, all_comps)
         return carry
 
-    lax.fori_loop(0, jnp.where(top, 2, 3), inner1, 0)
+    ready = jnp.where(top, 2, last)
+    lax.fori_loop(0, ready, inner1, 0)
     for k, step in enumerate(steps):
         if k > 1:
             pl.semaphore_wait(far_sem.at[k - 1], greeted(steps[k - 1]))
@@ -410,8 +417,8 @@
         fs = gs[0] + e2 * gs[2] + e1 * (gs[1] + gs[3]) + s1 * (gc[1] - gc[3])
         fourier = jnp.concatenate([fc, fs], axis=1)
         for p in range(lat):
-            for e in range(rad):
-                fsend[p * rad + e] = fourier[:, p * width + e * half:p * width + (e + 1) * half]
+            cols = slice(p * width, (p + 1) * width)
+            fsend[p * rad], fsend[p * rad + 1] = swap(fourier[:rows // 2, cols], fourier[rows // 2:, cols])
 
     pl.semaphore_wait(far_sem.at[len(steps) - 1], greeted(steps[-1]))
 
@@ -426,15 +433,6 @@
 
     def main(i, carry):
         s = order(i)
-
-        @pl.when(i == last)
-        def _():
-            arrived(u0.at[0, pl.ds(0, comps + 1), inner], r_recv.at[0])
-            lookup(facing)
-
-        @pl.when(jnp.logical_or(jnp.logical_and(top, i == 2), i == last))
-        def _():
-            inner1(i, 0)
 
         got_from(i, 1, *bulk)
         for side in sides:
@@ -447,8 +445,6 @@
         start_to(i, *later)
         return carry
 
-    lax.fori_loop(0, last, main, 0)
-
     def inner2(i, carry):
         s = order(i)
         alone = jnp.logical_and(top, i == 0)
@@ -464,6 +460,12 @@
                 sweep2(s, r, all_comps)
 
         return carry
+
+    lax.fori_loop(0, 2, main, 0)
+    arrived(u0.at[0, pl.ds(0, comps + 1), inner], r_recv.at[0])
+    lookup(facing)
+    lax.fori_loop(ready, shells, inner1, 0)
+    inner2(0, 0)
 
     for copy in c_tables[1:]:
         copy.wait()
@@ -480,15 +482,20 @@
     def _():
         arrived(frecv, all_recv.at[0])
 
-    spectrum = frecv[...].reshape(lat * rows, half)
-    sh, sl = split(spectrum)
+    packed = frecv[...].reshape(lat * rows // 2, width)
+    spectrum = jnp.concatenate([packed, pltpu.roll(packed, half, 1)], axis=0)
+    low = lax.broadcasted_iota(jnp.int32, spectrum.shape, 1) < half
+    sh = spectrum.astype(bf16).astype(f32)
+    both = jnp.where(low, sh, pltpu.roll(spectrum - sh, half, 1)).astype(bf16)
     down = (((0,), (0,)), ((), ()))
-    both = dot(jnp.concatenate([sh, sl], axis=1), cosine_v[0], down)
-    coef = both[:half] + both[half:] + dot(sh, cosine_v[1], down)
+    coef = dot(both, cosine_v[0], down)
+    coef = coef[:half] + coef[half:] + dot(both[:, :half], cosine_v[1], down)
     sh, sl = split(resp_t[...] * coef)
     nt = (((1,), (1,)), ((), ()))
-    load_rows = dot(cosine_v[0], sh, nt) + dot(cosine_v[0], sl, nt) + dot(cosine_v[1], sh, nt)
-    gsend[...] = load_rows.reshape(lat, rows, half)
+    load_rows = dot(cosine_v[0], jnp.concatenate([sh, sl], axis=0), nt)
+    load_rows = load_rows + pltpu.roll(load_rows, half, 1) + dot(cosine_v[1], jnp.concatenate([sh, sh], axis=0), nt)
+    upper, lower = load_rows[:lat * rows // 2], load_rows[lat * rows // 2:]
+    gsend[...] = jnp.where(low[:lat * rows // 2], upper, lower).reshape(lat, rows // 2, width)
     back = []
     for d, e in offsets:
         back.append(pltpu.make_async_remote_copy(
@@ -523,10 +530,11 @@
 
         return carry
 
-    main(last, 0)
+    lax.fori_loop(2, shells, main, 0)
     r_later.start()
 
-    lax.fori_loop(0, last, inner2, 0)
+    lax.fori_loop(1, last, inner2, 0)
+
 
     lax.fori_loop(0, shells, final, 0)
 
@@ -547,8 +555,8 @@
     arrived(grecv.at[pl.ds(0, blocks)], send_sem.at[5])
     arrived(grecv.at[pl.ds(0, blocks)], all_recv.at[1])
     for p in range(lat):
-        for e in range(rad):
-            gather[:, p * width + e * half:p * width + (e + 1) * half] = grecv[p * rad + e]
+        cols = slice(p * width, (p + 1) * width)
+        gather[:rows // 2, cols], gather[rows // 2:, cols] = swap(grecv[p * rad], grecv[p * rad + 1])
 
 
 def finish(out, coef, gather, trig, mask, out_h, coef_h, sea_h, sea, sem):
@@ -586,14 +594,16 @@
     comps, shells, rows, lon = disp.shape
     width = response.shape[1]
     trig = np.stack(longitude_quarter(lon, MODES))
-    cosine = np.stack(colatitude_table(lat * rows, MODES))
+    cosine = np.stack(colatitude_table(lat * rows, MODES)).reshape(2, lat, 2, rows // 2, MODES)
+    cosine = cosine.transpose(0, 2, 1, 3, 4).reshape(2, lat * rows, MODES)
     tables = [trig, cosine]
     hbm = pl.BlockSpec(memory_space=pltpu.HBM)
     vmem = pl.BlockSpec(memory_space=pltpu.VMEM)
     tall = rows + 2 * PAD
     field = pltpu.VMEM((comps, shells + 2, tall, lon), f32)
     half = width // rad
-    block = pltpu.VMEM((lat, rows, half), f32)
+    block = pltpu.VMEM((lat, rows // 2, width), f32)
+    blocks = pltpu.VMEM((lat * rad, rows // 2, width), f32)
     dma = pltpu.SemaphoreType.DMA
     spare = 4 * (disp.size + MODES * width // rad + 2 * rows * MODES + rows * lon) + 2 * trig.size + 65536
     out, coef, gather, trig_v, mask_v = pl.pallas_call(
@@ -613,7 +623,7 @@
             pltpu.VMEM((2, 1, lon), f32),
             pltpu.VMEM((shells + 2, tall, lon), jnp.int32),
             pltpu.VMEM((shells + 2, tall, lon), f32),
-            pltpu.VMEM((lat * rad, rows, half), f32), block, block, pltpu.VMEM((lat * rad, rows, half), f32),
+            blocks, block, block, blocks,
             pltpu.VMEM(response.shape, f32), pltpu.VMEM((half, MODES), f32),
             pltpu.VMEM(cosine.shape, bf16),
             pltpu.SMEM(visc.shape, f32),

time: 25.4 us -> 22.1 us (0.87)
  Pallas kernels: 24.7 us -> 21.4 us
    pallas_call x1, Pallas kernels: 22.8 us -> 19.5 us  [shards(): pl.pallas_call(functools.partial(kernel, lat, rad, visc.shape[0]), out_sh...]
where the time goes in v3:
time: 22.1 us; the launch traced here: 22 us
  Pallas kernels  21.4 us (97%)
  between operations  0.64 us (3%)
    pallas_call x1, Pallas kernels, shards(): pl.pallas_call(functools.partial(kernel, lat, rad, visc.shape[0]), out_sh...  19.5 us
    pallas_call x1, Pallas kernels, shards(): pl.pallas_call(finish, out_shape=tuple((jax.ShapeDtypeStruct(shape, f32)...  1.88 us

profile of v3, /device:TPU:0, one launch (start us, length us, event | category | flops | bytes accessed | tf_op | source)
XLA Modules:
  0.0 22.0 jit_solution(16700172129422964388)
XLA Ops:
  0.6 19.5 %shard_map.103 = (f32[3,4,32,2048]{3,2,1,0:T(8,128)S(1)}, f32[64,512]{1,0:T(8,128)S(1)}, f32[32,1024]{1,0:T(8,128)S(1)}, bf16[2,512,1024]{2,1,0:T(8,128)(2,1)S(1)}, s32[32,2048]{1,0:T(8,128)S(1)}) custom-call(f32[3,4,32,2048]{3,2,1,0:T(8,128)} %disp.1, f32[3,4,32,2048]{3,2,1,0:T(8,128)} %force.1, f32[16]{0:T(128)} %visc.1, s32[4,32,2048]{2,1,0:T(8,128)} %layer.1, ...), custom_call_target="tpu_custom_call" | custom-call | tf_op jit(solution)/shard_map/pallas_call | solution.py:609
  20.1 1.9 %shard_map.104 = (f32[3,4,32,2048]{3,2,1,0:T(8,128)}, f32[64,512]{1,0:T(8,128)}, f32[32,2048]{1,0:T(8,128)}) custom-call(f32[3,4,32,2048]{3,2,1,0:T(8,128)S(1)} %get-tuple-element.11.out, f32[64,512]{1,0:T(8,128)S(1)} %get-tuple-element.12.coef, f32[32,1024]{1,0:T(8,128)S(1)} %get-tuple-element.13.gather, bf16[2,512,1024]{2,1,0:T(8,128)(2,1)S(1)} %get-tuple-element.14.trig, ...), custom_call_target="tpu_custom_call" | custom-call | tf_op jit(solution)/shard_map/pallas_call | solution.py:636

commit v4 on v3

--- a/solution.py
+++ b/solution.py
@@ -98,6 +98,16 @@
         return {"lateral": peer(d), "radial": lax.rem(place + e, rad)}
 
     offsets = [(d, e) for d in reversed(range(lat)) for e in range(rad) if d or e]
+    quarters = max(1, lat // 4)
+    middle = jnp.logical_and(me >= quarters, me < lat - quarters)
+
+    def far_first(copies):
+        for here, rank in ((middle, [2, 3, 1, 0]), (jnp.logical_not(middle), [3, 2, 1, 0])):
+            @pl.when(here)
+            def _():
+                for _, copy in sorted(copies, key=lambda pair: rank.index(min(3, pair[0] // quarters))):
+                    copy.start()
+
     barrier = pltpu.get_barrier_semaphore()
     for e in range(1, rad):
         pl.semaphore_signal(barrier, inc=1, device_id=around(0, e), device_id_type=MESH)
@@ -119,8 +129,8 @@
 
     c_visc = load(visc, visc_s, 0)
     c_layer = load(layer, li.at[pl.ds(1, shells), inner], 1)
-    c_disp = load(disp, u0.at[:, pl.ds(1, shells), inner], 2)
-    c_force = load(force, fv, 3)
+    rest = pl.ds(1, comps - 1)
+    c_first = [load(disp.at[0], u0.at[0, pl.ds(1, shells), inner], 2), load(force.at[0], fv.at[0], 3)]
 
     void = jnp.where(top, shells + 1, 0)
     tall, wide = rows + 2 * PAD, (1, lon)
@@ -167,8 +177,6 @@
         ]
         return [lateral(side, 0, a, b) for a, b in refs]
 
-    rest = pl.ds(1, comps - 1)
-
     def bulk_rest(side, i):
         s = order(i)
         return [lateral(side, 1 + i, disp.at[rest, s, side[4]], u0.at[rest, s + 1, side[6]])]
@@ -266,6 +274,7 @@
 
     r_layer.start()
     r_disp.start()
+    c_rest = [load(disp.at[rest], u0.at[rest, pl.ds(1, shells), inner], 4), load(force.at[rest], fv.at[rest], 5)]
     greet(far_sem.at[0], steps[0])
 
     c_visc.wait()
@@ -290,13 +299,11 @@
         pl.semaphore_wait(far_sem.at[0], greeted(steps[0]))
         greet(far_sem.at[1], steps[1])
 
-    c_disp.wait()
-    c_force.wait()
+    tables = [(trig, trig_v), (response, resp_v), (cosine, cosine_v), (mask, mask_v)]
+    for copy in c_first:
+        copy.wait()
+    c_tables = [load(a, b, 6 + k) for k, (a, b) in enumerate(tables)]
     start_to(1, *bulk)
-    tables = [(trig, trig_v), (response, resp_v), (cosine, cosine_v), (mask, mask_v)]
-    c_tables = [load(a, b, 4 + k) for k, (a, b) in enumerate(tables)]
-
-    start_to(2, *bulk)
 
     chunk = lon // 4
 
@@ -334,11 +341,11 @@
                 total = total + ws[5] * right
                 store(c, lanes, 0.2 * u + rate * total)
 
-    def sweep1(s, r, some):
+    def sweep1(s, r, some, size=8):
         def store(c, lanes, value):
-            u1[c, s + 1, PAD + r:PAD + r + 8, lanes] = value
-
-        sweep(u0, s, PAD + r, 8, some, lambda c, lanes: fv[c, s, r:r + 8, lanes], store)
+            u1[c, s + 1, PAD + r:PAD + r + size, lanes] = value
+
+        sweep(u0, s, PAD + r, size, some, lambda c, lanes: fv[c, s, r:r + size, lanes], store)
 
     def sweep2(s, r, some):
         def store(c, lanes, value):
@@ -356,8 +363,33 @@
             sweep1(s, r, all_comps)
         return carry
 
-    ready = jnp.where(top, 2, last)
-    lax.fori_loop(0, ready, inner1, 0)
+    def inner1_first(i, carry):
+        for r in inner_rows:
+            sweep1(last - i, r, [0])
+        sweep1(last - i, 1, [0], 7)
+        sweep1(last - i, rows - 8, [0], 7)
+        return carry
+
+    def inner1_rest(i, carry):
+        for r in inner_rows:
+            sweep1(last - i, r, rest_comps)
+        return carry
+
+    @pl.when(top)
+    def _():
+        lax.fori_loop(0, 2, inner1_first, 0)
+        for r in inner_rows:
+            sweep2(last, r, [0])
+
+    @pl.when(jnp.logical_not(top))
+    def _():
+        for copy in c_rest:
+            copy.wait()
+        lax.fori_loop(0, last, inner1, 0)
+
+    for i in range(2, shells):
+        start_to(i, *bulk)
+
     for k, step in enumerate(steps):
         if k > 1:
             pl.semaphore_wait(far_sem.at[k - 1], greeted(steps[k - 1]))
@@ -388,8 +420,8 @@
                 lookup_at(shells - 1, side[6])
 
         def early(i, carry):
-            for r in edge_rows:
-                sweep1(last - i, r, [0])
+            for r in (0, rows - 1):
+                sweep1(last - i, r, [0], 1)
             return carry
 
         lax.fori_loop(0, 2, early, 0)
@@ -401,7 +433,7 @@
 
                 sweep(u0, last, row, 1, [0], lambda c, lanes: fh[side[0], :, lanes], store)
 
-        for r in range(0, rows, 8):
+        for r in edge_rows:
             sweep2(last, r, [0])
 
     c_tables[0].wait()
@@ -410,7 +442,8 @@
     def _():
         x = jnp.concatenate([out[0, last, :, quarter * m:quarter * (m + 1)] for m in range(4)], axis=0)
         xh, xl = split(x)
-        g = dot(xh, trig_v[0]) + dot(xl, trig_v[0]) + dot(xh, trig_v[1])
+        g = dot(jnp.concatenate([xh, xl], axis=0), trig_v[0])
+        g = g[:4 * rows] + g[4 * rows:] + dot(xh, trig_v[1])
         gc = [g[rows * m:rows * (m + 1), :modes] for m in range(4)]
         gs = [g[rows * m:rows * (m + 1), modes:] for m in range(4)]
         fc = gc[0] + e2 * gc[2] + e1 * (gc[1] + gc[3]) - s1 * (gs[1] - gs[3])
@@ -424,12 +457,12 @@
 
     @pl.when(top)
     def _():
-        for _, _, copy in forward:
-            copy.start()
+        far_first([(d, copy) for d, _, copy in forward])
         frecv[me] = fsend[me * rad + rad - 1]
 
-    for i in range(3, shells):
-        start_to(i, *bulk)
+        for copy in c_rest:
+            copy.wait()
+
 
     def main(i, carry):
         s = order(i)
@@ -461,10 +494,15 @@
 
         return carry
 
-    lax.fori_loop(0, 2, main, 0)
+    ahead = jnp.where(top, last, 2)
+    lax.fori_loop(0, ahead, main, 0)
     arrived(u0.at[0, pl.ds(0, comps + 1), inner], r_recv.at[0])
     lookup(facing)
-    lax.fori_loop(ready, shells, inner1, 0)
+    @pl.when(top)
+    def _():
+        lax.fori_loop(0, 2, inner1_rest, 0)
+
+    lax.fori_loop(jnp.where(top, 2, last), shells, inner1, 0)
     inner2(0, 0)
 
     for copy in c_tables[1:]:
@@ -498,12 +536,11 @@
     gsend[...] = jnp.where(low[:lat * rows // 2], upper, lower).reshape(lat, rows // 2, width)
     back = []
     for d, e in offsets:
-        back.append(pltpu.make_async_remote_copy(
+        back.append((d, pltpu.make_async_remote_copy(
             src_ref=gsend.at[peer(d)], dst_ref=grecv.at[me * rad + place],
             send_sem=send_sem.at[5], recv_sem=all_recv.at[1],
-            device_id=around(d, e), device_id_type=MESH))
-    for copy in back:
-        copy.start()
+            device_id=around(d, e), device_id_type=MESH)))
+    far_first(back)
     grecv[me * rad + place] = gsend[me]
     coef_out[...] = coef
 
@@ -530,7 +567,7 @@
 
         return carry
 
-    lax.fori_loop(2, shells, main, 0)
+    lax.fori_loop(ahead, shells, main, 0)
     r_later.start()
 
     lax.fori_loop(1, last, inner2, 0)
@@ -580,7 +617,8 @@
     a = jnp.concatenate([jnp.concatenate(pair, axis=1) for pair in twisted], axis=0)
     ah, al = split(a)
     nt = (((1,), (1,)), ((), ()))
-    total = dot(ah, trig[0], nt) + dot(al, trig[0], nt) + dot(ah, trig[1], nt)
+    total = dot(jnp.concatenate([ah, al], axis=0), trig[0], nt)
+    total = total[:4 * rows] + total[4 * rows:] + dot(ah, trig[1], nt)
     for m in range(4):
         cut = slice(quarter * m, quarter * (m + 1))
         sea[:, cut] = mask[:, cut].astype(f32) * total[rows * m:rows * (m + 1)]
@@ -627,7 +665,7 @@
             pltpu.VMEM(response.shape, f32), pltpu.VMEM((half, MODES), f32),
             pltpu.VMEM(cosine.shape, bf16),
             pltpu.SMEM(visc.shape, f32),
-            dma((8,)), dma((6,)), dma((2, 1 + 2 * shells)), dma((2,)), dma((2,)),
+            dma((10,)), dma((6,)), dma((2, 1 + 2 * shells)), dma((2,)), dma((2,)),
             pltpu.SemaphoreType.REGULAR((max(1, (lat - 1).bit_length()),)),
         ],
         compiler_params=pltpu.CompilerParams(

time: 22.1 us -> 21.9 us (level)
  Pallas kernels: 21.4 us -> 21.1 us
where the time goes in v4:
time: 21.9 us; the launch traced here: 21.7 us
  Pallas kernels  21.1 us (96%)
  between operations  0.64 us (3%)
    pallas_call x1, Pallas kernels, shards(): pl.pallas_call(functools.partial(kernel, lat, rad, visc.shape[0]), out_sh...  19.3 us
    pallas_call x1, Pallas kernels, shards(): pl.pallas_call(finish, out_shape=tuple((jax.ShapeDtypeStruct(shape, f32)...  1.83 us

profile of v4, /device:TPU:0, one launch (start us, length us, event | category | flops | bytes accessed | tf_op | source)
XLA Modules:
  0.0 21.7 jit_solution(12917425118840907161)
XLA Ops:
  0.6 19.3 %shard_map.103 = (f32[3,4,32,2048]{3,2,1,0:T(8,128)S(1)}, f32[64,512]{1,0:T(8,128)S(1)}, f32[32,1024]{1,0:T(8,128)S(1)}, bf16[2,512,1024]{2,1,0:T(8,128)(2,1)S(1)}, s32[32,2048]{1,0:T(8,128)S(1)}) custom-call(f32[3,4,32,2048]{3,2,1,0:T(8,128)} %disp.1, f32[3,4,32,2048]{3,2,1,0:T(8,128)} %force.1, f32[16]{0:T(128)} %visc.1, s32[4,32,2048]{2,1,0:T(8,128)} %layer.1, ...), custom_call_target="tpu_custom_call" | custom-call | tf_op jit(solution)/shard_map/pallas_call | solution.py:647
  19.9 1.8 %shard_map.104 = (f32[3,4,32,2048]{3,2,1,0:T(8,128)}, f32[64,512]{1,0:T(8,128)}, f32[32,2048]{1,0:T(8,128)}) custom-call(f32[3,4,32,2048]{3,2,1,0:T(8,128)S(1)} %get-tuple-element.11.out, f32[64,512]{1,0:T(8,128)S(1)} %get-tuple-element.12.coef, f32[32,1024]{1,0:T(8,128)S(1)} %get-tuple-element.13.gather, bf16[2,512,1024]{2,1,0:T(8,128)(2,1)S(1)} %get-tuple-element.14.trig, ...), custom_call_target="tpu_custom_call" | custom-call | tf_op jit(solution)/shard_map/pallas_call | solution.py:674

commit v5 on v4

--- a/solution.py
+++ b/solution.py
@@ -299,7 +299,7 @@
         pl.semaphore_wait(far_sem.at[0], greeted(steps[0]))
         greet(far_sem.at[1], steps[1])
 
-    tables = [(trig, trig_v), (response, resp_v), (cosine, cosine_v), (mask, mask_v)]
+    tables = [(response, resp_v), (trig, trig_v), (cosine, cosine_v), (mask, mask_v)]
     for copy in c_first:
         copy.wait()
     c_tables = [load(a, b, 6 + k) for k, (a, b) in enumerate(tables)]
@@ -410,6 +410,12 @@
             send_sem=send_sem.at[4], recv_sem=all_recv.at[0],
             device_id={"lateral": peer(d), "radial": e}, device_id_type=MESH)))
 
+    c_tables[0].wait()
+    answer = resp_v[:, :half]
+    for e in range(1, rad):
+        answer = jnp.where(place == e, resp_v[:, e * half:(e + 1) * half], answer)
+    resp_t[...] = answer.T
+
     @pl.when(top)
     def _():
         for side in sides:
@@ -436,7 +442,7 @@
         for r in edge_rows:
             sweep2(last, r, [0])
 
-    c_tables[0].wait()
+    c_tables[1].wait()
 
     @pl.when(top)
     def _():
@@ -505,12 +511,8 @@
     lax.fori_loop(jnp.where(top, 2, last), shells, inner1, 0)
     inner2(0, 0)
 
-    for copy in c_tables[1:]:
+    for copy in c_tables[2:]:
         copy.wait()
-    answer = resp_v[:, :half]
-    for e in range(1, rad):
-        answer = jnp.where(place == e, resp_v[:, e * half:(e + 1) * half], answer)
-    resp_t[...] = answer.T
 
     @pl.when(top)
     def _():

time: 21.9 us -> 21.9 us (level)
  no operation moved by 1% of the time
where the time goes in v5:
time: 21.9 us; the launch traced here: 21.7 us
  Pallas kernels  21.1 us (96%)
  between operations  0.64 us (3%)
    pallas_call x1, Pallas kernels, shards(): pl.pallas_call(functools.partial(kernel, lat, rad, visc.shape[0]), out_sh...  19.3 us
    pallas_call x1, Pallas kernels, shards(): pl.pallas_call(finish, out_shape=tuple((jax.ShapeDtypeStruct(shape, f32)...  1.83 us

profile of v5, /device:TPU:0, one launch (start us, length us, event | category | flops | bytes accessed | tf_op | source)
XLA Modules:
  0.0 21.7 jit_solution(2718143232277622488)
XLA Ops:
  0.6 19.3 %shard_map.103 = (f32[3,4,32,2048]{3,2,1,0:T(8,128)S(1)}, f32[64,512]{1,0:T(8,128)S(1)}, f32[32,1024]{1,0:T(8,128)S(1)}, bf16[2,512,1024]{2,1,0:T(8,128)(2,1)S(1)}, s32[32,2048]{1,0:T(8,128)S(1)}) custom-call(f32[3,4,32,2048]{3,2,1,0:T(8,128)} %disp.1, f32[3,4,32,2048]{3,2,1,0:T(8,128)} %force.1, f32[16]{0:T(128)} %visc.1, s32[4,32,2048]{2,1,0:T(8,128)} %layer.1, ...), custom_call_target="tpu_custom_call" | custom-call | tf_op jit(solution)/shard_map/pallas_call | solution.py:649
  19.9 1.8 %shard_map.104 = (f32[3,4,32,2048]{3,2,1,0:T(8,128)}, f32[64,512]{1,0:T(8,128)}, f32[32,2048]{1,0:T(8,128)}) custom-call(f32[3,4,32,2048]{3,2,1,0:T(8,128)S(1)} %get-tuple-element.11.out, f32[64,512]{1,0:T(8,128)S(1)} %get-tuple-element.12.coef, f32[32,1024]{1,0:T(8,128)S(1)} %get-tuple-element.13.gather, bf16[2,512,1024]{2,1,0:T(8,128)(2,1)S(1)} %get-tuple-element.14.trig, ...), custom_call_target="tpu_custom_call" | custom-call | tf_op jit(solution)/shard_map/pallas_call | solution.py:676
